TPU v7x, 256 devices: a whole 4x4x8 slice. The times are simulated.
256 devices in a mesh: ctx: 16 (over y_hi, z), head: 8 (over x, core), rep: 2 (over y_lo).
Axes of the slice: x: 4, y: 4 (y_hi: 2, y_lo: 2; y = y_hi * 2 + y_lo), z: 8, core: 2. Of those that a mesh axis runs over, the one named last changes fastest.
Arguments:
- query_latent: bfloat16 [8192, 1536], P(('rep', 'ctx')), parts along dimension 0, may hold values from -6 to 6
- key_rows: bfloat16 [8192, 576], P(('rep', 'ctx')), parts along dimension 0, may hold values from -640 to 640
- key_cache: bfloat16 [1024, 576], P('rep'), parts along dimension 0, may hold values from -640 to 640
- prompt_start: int32 [2], P('rep'), parts along dimension 0, may hold values from 0 to 512
- w_query: bfloat16 [1536, 12288], P(None, 'head'), may hold values from -0.15625 to 0.15625
- w_key_up: bfloat16 [64, 128, 512], P('head'), may hold values from -0.5 to 0.5
- w_value_up: bfloat16 [64, 512, 128], P('head'), may hold values from -0.25 to 0.25
- w_output: bfloat16 [64, 128, 7168], P('head', 'ctx'), may hold values from -0.09375 to 0.09375
Outputs:
- layer_out: bfloat16 [8192, 7168], P(('rep', 'ctx'), 'head'), parts along dimension 0
There are 2 independent parts, one for each index of `rep`. A program takes and returns all parts, laid end to end along the dimension named above; an argument that names none is the same for every part. Nothing has to cross between parts.
All inputs are finite; a program needn't handle non-finite values.
Results may differ from a plain program's by a relative error of at most 0.017.
The roundings to bfloat16 on the way count: a program that leaves them out, or rounds other values in their place, can miss the bound.
Values may be sent and summed in bfloat16 or wider, within the bound.
No kernel may reach another device: no remote copies, remote signals or barrier semaphores. Data moves between devices by JAX's collectives and lax.ppermute only.
A program may use at most 128 MiB of HBM per device.

v0:
```python
import jax
import jax.numpy as jnp
from jax import lax
from jax.sharding import PartitionSpec as P


def passed_along(x, axis, by):
    devices = lax.axis_size(axis)
    pairs = [(i, i + by) for i in range(devices) if 0 <= i + by < devices]
    return lax.ppermute(x, axis, pairs)


def rotate(values, positions):
    half_dim = values.shape[-1] // 2
    inverse = jnp.power(
        jnp.float32(10000.0), -jnp.arange(half_dim, dtype=jnp.float32) * (2.0 / values.shape[-1])
    )
    angles = positions[..., None] * inverse
    cosine = jnp.cos(angles)
    sines = jnp.sin(angles)
    lower_half = values[..., :half_dim]
    upper_half = values[..., half_dim:]
    return jnp.concatenate(
        [lower_half * cosine - upper_half * sines, lower_half * sines + upper_half * cosine], -1
    )


def local(query_latent, key_rows, key_cache, prompt_start, w_query, w_key_up, w_value_up, w_output):
    tok_rows = query_latent.shape[0]
    heads_dev, nope_dim, latent = w_key_up.shape
    rope_dim = key_rows.shape[1] - latent
    window = key_cache.shape[0]
    slab_index = lax.axis_index("ctx")
    queries = jnp.dot(query_latent, w_query, preferred_element_type=jnp.float32).astype(
        jnp.bfloat16
    )
    queries = queries.reshape(tok_rows, heads_dev, nope_dim + rope_dim)
    query_lat = jnp.einsum(
        "thn,hnl->thl", queries[..., :nope_dim], w_key_up, preferred_element_type=jnp.float32
    ).astype(jnp.bfloat16)
    token_pos = (slab_index * tok_rows + jnp.arange(tok_rows, dtype=jnp.int32)).astype(jnp.float32)
    query_rot = rotate(queries[..., nope_dim:].astype(jnp.float32), token_pos[:, None]).astype(
        jnp.bfloat16
    )
    key_rot = rotate(key_rows[:, latent:].astype(jnp.float32), token_pos).astype(jnp.bfloat16)
    own_keys = jnp.concatenate([key_rows[:, :latent], key_rot], 1)
    piece_rows = min(tok_rows, window)
    hop_count = window // piece_rows
    received = []
    for hop_number in range(hop_count):
        received.append(passed_along(own_keys, "ctx", hop_number + 1))
    key_blocks = []
    for hop_number in range(hop_count):
        distance = hop_number + 1
        cache_slot = jnp.clip(hop_count - distance + slab_index, 0, hop_count - 1)
        cached = lax.dynamic_slice_in_dim(key_cache, cache_slot * piece_rows, piece_rows, 0)
        key_blocks.append(jnp.where(slab_index < distance, cached, received[hop_number]))
    all_keys = jnp.concatenate(key_blocks[::-1] + [own_keys], 0)
    key_span = all_keys.shape[0]
    key_lat = all_keys[:, :latent]
    score_scale = (nope_dim + rope_dim) ** (-0.5)
    scores = jnp.einsum("thl,kl->htk", query_lat, key_lat, preferred_element_type=jnp.float32)
    scores = scores + jnp.einsum(
        "thr,kr->htk", query_rot, all_keys[:, latent:], preferred_element_type=jnp.float32
    )
    scores = scores * score_scale
    key_pos = jnp.arange(key_span, dtype=jnp.int32) - window
    row_ids = jnp.arange(tok_rows, dtype=jnp.int32)
    relative = key_pos[None, :] - row_ids[:, None]
    in_prompt = slab_index * tok_rows + key_pos >= -prompt_start[0]
    visible = (relative <= 0) & (relative > -window) & in_prompt[None, :]
    scores = jnp.where(visible[None], scores, -1e30)
    row_max = jnp.max(scores, axis=-1, keepdims=True)
    powers = jnp.exp(scores - row_max)
    weights = (powers / jnp.sum(powers, axis=-1, keepdims=True)).astype(jnp.bfloat16)
    mixed_lat = jnp.einsum(
        "htk,kl->thl", weights, key_lat, preferred_element_type=jnp.float32
    ).astype(jnp.bfloat16)
    attention = jnp.einsum(
        "thl,hlv->thv", mixed_lat, w_value_up, preferred_element_type=jnp.float32
    ).astype(jnp.bfloat16)
    full_rows = lax.all_gather(w_output, "ctx", axis=1, tiled=True)
    flat_attention = attention.reshape(tok_rows, -1)
    flat_rows = full_rows.reshape(-1, full_rows.shape[2])
    partial_value = jnp.dot(flat_attention, flat_rows, preferred_element_type=jnp.float32)
    return lax.psum_scatter(partial_value, "head", scatter_dimension=1, tiled=True).astype(
        jnp.bfloat16
    )


def solution(mesh):
    return jax.shard_map(
        local,
        mesh=mesh,
        in_specs=(
            P(("rep", "ctx"), None),
            P(("rep", "ctx"), None),
            P("rep", None),
            P("rep"),
            P(None, "head"),
            P("head", None, None),
            P("head", None, None),
            P("head", "ctx", None),
        ),
        out_specs=P(("rep", "ctx"), "head"),
        check_vma=False,
    )
```

profile of v0, /device:TPU:1, one launch (start us, length us, event | category | flops | bytes accessed | tf_op | source)
XLA Modules:
  0.0 288.0 jit_solution(6459296274716134943)
XLA Ops:
  6.5 0.7 all-gather.2.cloned.1.call-update
  7.3 0.0 reduce-scatter.2.cloned.1.call-start
  7.3 1.0 slice.30
  8.3 0.8 slice_convert_fusion.1
  9.1 0.2 multiply_cosine_fusion
  9.3 0.1 copy.27
  9.4 0.1 copy.28
  9.5 0.1 copy.43
  9.7 0.8 pad_maximum_fusion
  10.5 6.4 %collective-permute-start = (bf16[256,576]{1,0:T(8,128)(2,1)}, bf16[256,576]{1,0:T(8,128)(2,1)}, u32[]{:S(2)}, u32[]{:S(2)}) collective-permute-start(bf16[256,576]{1,0:T(8,128)(2,1)} %pad_maximum_fusion), channel_id=1, source_target_pairs={{0,32},{16,48},{32,64},{48,80},{64,96},{80,112},{96,128},{112,144}... | collective-permute-start | bytes 884744 | tf_op jit(solution)/shard_map/ppermute | solution.py:10
  16.9 4.3 %collective-permute-start.1 = (bf16[256,576]{1,0:T(8,128)(2,1)}, bf16[256,576]{1,0:T(8,128)(2,1)}, u32[]{:S(2)}, u32[]{:S(2)}) collective-permute-start(bf16[256,576]{1,0:T(8,128)(2,1)} %pad_maximum_fusion), channel_id=1, source_target_pairs={{0,16},{16,32},{32,48},{48,64},{64,80},{80,96},{96,112},{112,128},... | collective-permute-start | bytes 884744 | tf_op jit(solution)/shard_map/ppermute | solution.py:10
  21.2 4.0 %convolution_convert_fusion = bf16[256,1536]{1,0:T(8,128)(2,1)S(1)} fusion(bf16[256,1536]{1,0:T(8,128)(2,1)} %param.8, bf16[1536,1536]{1,0:T(8,128)(2,1)} %param.12), kind=kOutput, calls=%fused_computation.6 | convolution fusion | flops 1208352768 | bytes 6291456 | tf_op jit(solution)/shard_map/dot_general | solution.py:34
  25.2 0.3 copy.30
  26.2 0.7 subtract_convert_fusion
  26.9 0.3 fusion.18
  27.2 1.1 constant_dynamic-slice_fusion.1
  28.4 0.2 copy.42
  28.6 0.2 copy.44
  28.8 0.1 broadcast_select_fusion.1
  28.8 11.8 %collective-permute-done.1 = bf16[256,576]{1,0:T(8,128)(2,1)} collective-permute-done((bf16[256,576]{1,0:T(8,128)(2,1)}, bf16[256,576]{1,0:T(8,128)(2,1)}, u32[]{:S(2)}, u32[]{:S(2)}) %collective-permute-start.1) | collective-permute-done | bytes 294944 | tf_op jit(solution)/shard_map/ppermute | solution.py:10
  40.7 1.1 maximum_maximum_fusion
  41.8 6.1 %fusion.2 = f32[768,256,8]{1,0,2:T(8,128)} fusion(bf16[8,128,512]{2,1,0:T(8,128)(2,1)S(1)} %copy-done, bf16[768,576]{1,0:T(8,128)(2,1)} %maximum_maximum_fusion, bf16[256,8,192]{0,2,1:T(8,128)(2,1)S(1)} %bitcast.29), kind=kOutput, calls=%fused_computation.7 | convolution fusion | flops 1880096768 | bytes 8650752 | tf_op jit(solution)/shard_map/thl,kl->htk/dot_general | solution.py:62
  47.9 4.0 %bitcast_select_fusion = f32[8,256,768]{1,2,0:T(8,128)S(1)} fusion(f32[768,256,8]{1,0,2:T(8,128)} %fusion.2, pred[256,768]{0,1:T(8,128)(4,1)S(1)} %fusion.18, bf16[256,8,32]{0,2,1:T(8,128)(2,1)S(1)} %copy-done.3, bf16[256,8,32]{0,2,1:T(8,128)(2,1)S(1)} %get-tuple-element.5, bf16[256,32]{1,0:T(8,128)(2,1)S(1)} %copy.28, ...), kind=kOutput, calls=%fused_computation.2 | convolution fusion | flops 207060992 | bytes 13926400 | tf_op jit(solution)/shard_map/thr,kr->htk/dot_general | solution.py:63
  52.0 2.6 copy-done.1
  54.5 1.1 fusion.35
  55.7 0.1 copy-done.2
  55.8 7.8 %fusion.12 = bf16[256,8,128]{2,0,1:T(8,128)(2,1)S(1)} fusion(bf16[8,512,128]{2,1,0:T(8,128)(2,1)} %param.14, f32[8,256]{1,0:T(8,128)S(1)} %fusion.35, bf16[768,576]{1,0:T(8,128)(2,1)S(1)} %copy-done.2, f32[8,256,768]{1,2,0:T(8,128)} %copy-done.1), kind=kOutput, calls=%fused_computation.14 | convolution fusion | flops 1885080320 | bytes 14950400 | tf_op jit(solution)/shard_map/thl,hlv->thv/dot_general | solution.py:79
  63.5 159.8 %all-gather.2.cloned.1.call-done = bf16[8,128,7168]{2,1,0:T(8,128)(2,1)} async-done(((bf16[8,8,7168]{2,1,0:T(8,128)(2,1)}), bf16[8,128,7168]{2,1,0:T(8,128)(2,1)}) %all-gather.2.cloned.1.call-update) | async-done | bytes 14680080 | tf_op jit(solution)/shard_map/all_gather | solution.py:82
  223.3 9.1 %convolution_bitcast_fusion = f32[256,7168]{1,0:T(8,128)} fusion(bf16[256,8,128]{2,0,1:T(8,128)(2,1)S(1)} %fusion.12, bf16[8,128,7168]{2,1,0:T(8,128)(2,1)} %all-gather.2.cloned.1.call-done), kind=kOutput, calls=%fused_computation.1 | convolution fusion | flops 3758096384 | bytes 22544384 | tf_op jit(solution)/shard_map/dot_general | solution.py:85
  232.4 0.0 reduce-scatter.2.cloned.1.call-update
  232.4 46.8 %reduce-scatter.2.cloned.1.call-done = f32[256,896]{1,0:T(8,128)} async-done(((f32[256,7168]{1,0:T(8,128)}), f32[256,896]{1,0:T(8,128)}) %reduce-scatter.2.cloned.1.call-update) | async-done | bytes 917520 | tf_op jit(solution)/shard_map/reduce_scatter | solution.py:86
  279.2 2.0 convert_element_type.54
  (14 shorter events, 0.1 us)
Async XLA Ops:
  6.5 35.3 %copy-start = (bf16[8,128,512]{2,1,0:T(8,128)(2,1)S(1)}, bf16[8,128,512]{2,1,0:T(8,128)(2,1)}, u32[]{:S(2)}) copy-start(bf16[8,128,512]{2,1,0:T(8,128)(2,1)} %param.13) | copy-start | bytes 3145732
  6.5 216.8 %all-gather.2.cloned.1.call-start = ((), (), s32[]{:S(2)}) async-start(), calls=%async_computation.1 | async-start | bytes 15597568 | tf_op jit(solution)/shard_map/all_gather | solution.py:82
  7.3 271.9 %reduce-scatter.2.cloned.1.call-start = ((), (), s32[]{:S(2)}) async-start(), calls=%async_computation.2 | async-start | bytes 8257536 | tf_op jit(solution)/shard_map/reduce_scatter | solution.py:86
  10.5 18.3 %collective-permute-start = (bf16[256,576]{1,0:T(8,128)(2,1)}, bf16[256,576]{1,0:T(8,128)(2,1)}, u32[]{:S(2)}, u32[]{:S(2)}) collective-permute-start(bf16[256,576]{1,0:T(8,128)(2,1)} %pad_maximum_fusion), channel_id=1, source_target_pairs={{0,32},{16,48},{32,64},{48,80},{64,96},{80,112},{96,128},{112,144}... | collective-permute-start | bytes 884744 | tf_op jit(solution)/shard_map/ppermute | solution.py:10
  16.9 23.7 %collective-permute-start.1 = (bf16[256,576]{1,0:T(8,128)(2,1)}, bf16[256,576]{1,0:T(8,128)(2,1)}, u32[]{:S(2)}, u32[]{:S(2)}) collective-permute-start(bf16[256,576]{1,0:T(8,128)(2,1)} %pad_maximum_fusion), channel_id=1, source_target_pairs={{0,16},{16,32},{32,48},{48,64},{64,80},{80,96},{96,112},{112,128},... | collective-permute-start | bytes 884744 | tf_op jit(solution)/shard_map/ppermute | solution.py:10
  40.7 7.2 %copy-start.3 = (bf16[256,8,32]{0,2,1:T(8,128)(2,1)S(1)}, bf16[256,8,32]{0,2,1:T(8,128)(2,1)}, u32[]{:S(2)}) copy-start(bf16[256,8,32]{0,2,1:T(8,128)(2,1)} %get-tuple-element.6) | copy-start | bytes 393220
  52.0 2.6 copy-start.1
  54.5 1.2 copy-start.2
Sparse Core Ops, SparseCore 0:
  10.0 213.2 all-gather.1
  232.5 46.6 reduce-scatter.1
where the time goes:
time: 289 us; the launch traced here: 288 us
  waiting for transfers between devices  219 us (76%)
  matrix products  30.9 us (11%)
  between operations  14.2 us (5%)
  starting transfers between devices  10.8 us (4%)
  other arithmetic  7.18 us (2%)
  local copies, waits for them, and re-layouts  5.8 us (2%)
    all_gather x1, waiting for transfers between devices, local(): full_rows = lax.all_gather(w_output, 'ctx', axis=1, tiled=True)  160 us
    reduce_scatter x1, waiting for transfers between devices, local(): lax.psum_scatter(partial_value, 'head', scatter_dimension=1, tiled=True)  46.8 us
    ppermute x2, waiting for transfers between devices, passed_along(): return lax.ppermute(x, axis, pairs)  11.8 us
    ppermute x2, starting transfers between devices, passed_along(): return lax.ppermute(x, axis, pairs)  10.7 us
    dot_general x1, matrix products, local(): jnp.dot(flat_attention, flat_rows, preferred_element_type=jnp.float32)  9.08 us
    dot_general x1, matrix products, local(): jnp.einsum('thl,hlv->thv', mixed_lat, w_value_up, preferred_element_type=...  7.75 us
    dot_general x1, matrix products, local(): jnp.einsum('thl,kl->htk', query_lat, key_lat, preferred_element_type=jnp....  6.09 us
  transfers between devices with their start and end apart: 4, of which 3 were waited for; matrix products, arithmetic and copies ran while one was open for 10% of the time, Pallas kernels for 0%

commit v1 on v0

--- a/solution.py
+++ b/solution.py
@@ -79,7 +79,9 @@
     attention = jnp.einsum(
         "thl,hlv->thv", mixed_lat, w_value_up, preferred_element_type=jnp.float32
     ).astype(jnp.bfloat16)
-    full_rows = lax.all_gather(w_output, "ctx", axis=1, tiled=True)
+    full_rows = jnp.concatenate(
+        lax.all_to_all(jnp.stack([w_output] * lax.axis_size("ctx")), "ctx", 0, 0), axis=1
+    )
     flat_attention = attention.reshape(tok_rows, -1)
     flat_rows = full_rows.reshape(-1, full_rows.shape[2])
     partial_value = jnp.dot(flat_attention, flat_rows, preferred_element_type=jnp.float32)

time: 289 us -> 487 us (1.69)
  waiting for transfers between devices: 219 us -> 395 us
  local copies, waits for them, and re-layouts: 5.8 us -> 22.2 us
  starting transfers between devices: 10.8 us -> 19.9 us
    ppermute x2, waiting for transfers between devices: 11.8 us -> 329 us  [passed_along(): return lax.ppermute(x, axis, pairs)]
    all_gather x1 -> x0, waiting for transfers between devices: 160 us -> none  [local(): full_rows = lax.all_gather(w_output, 'ctx', axis=1, tiled=True)]
    reduce_scatter x1, waiting for transfers between devices: 46.8 us -> 66.1 us  [local(): lax.psum_scatter(partial_value, 'head', scatter_dimension=1, tiled=True)]
    all_to_all x0 -> x1, starting transfers between devices: none -> 11.9 us  [local(): lax.all_to_all(jnp.stack([w_output] * lax.axis_size('ctx')), 'ctx', 0, 0)]
    another operation x2 -> x3, local copies, waits for them, and re-layouts: 0.24 us -> 8.56 us  [the longest x1 8.32 us: local(): jnp.stack([w_output] * lax.axis_size('ctx'))]
    all_to_all x0 -> x1, local copies, waits for them, and re-layouts: none -> 7.58 us  [local(): lax.all_to_all(jnp.stack([w_output] * lax.axis_size('ctx')), 'ctx', 0, 0)]
  transfers between devices with their start and end apart: 4 -> 4, of which waited for: 3 -> 2; matrix products, arithmetic and copies ran while one was open for 10% -> 6% of each run, Pallas kernels for 0% -> 0%
where the time goes in v1:
time: 487 us
  waiting for transfers between devices  395 us (81%)
  matrix products  28.5 us (6%)
  local copies, waits for them, and re-layouts  22.2 us (5%)
  starting transfers between devices  19.9 us (4%)
  between operations  14.3 us (3%)
  other arithmetic  6.42 us (1%)
    ppermute x2, waiting for transfers between devices, passed_along(): return lax.ppermute(x, axis, pairs)  329 us
    reduce_scatter x1, waiting for transfers between devices, local(): lax.psum_scatter(partial_value, 'head', scatter_dimension=1, tiled=True)  66.1 us
    all_to_all x1, starting transfers between devices, local(): lax.all_to_all(jnp.stack([w_output] * lax.axis_size('ctx')), 'ctx', 0, 0)  11.9 us
  transfers between devices with their start and end apart: 4, of which 2 were waited for; matrix products, arithmetic and copies ran while one was open for 6% of the time, Pallas kernels for 0%

profile of v1, /device:TPU:1, one launch (start us, length us, event | category | flops | bytes accessed | tf_op | source)
XLA Modules:
  0.0 486.6 jit_solution(13942027453409324577)
XLA Ops:
  6.5 8.3 %stack.2 = bf16[16,8,8,7168]{3,2,1,0:T(8,128)(2,1)} broadcast(bf16[8,8,7168]{2,1,0:T(8,128)(2,1)} %param.15), dimensions={1,2,3} | broadcast | bytes 15597568 | tf_op jit(solution)/shard_map/stack | solution.py:83
  14.9 11.9 %all-to-all-start = ((bf16[16,8,8,7168]{3,2,1,0:T(8,128)(2,1)}), bf16[16,8,8,7168]{3,2,1,0:T(8,128)(2,1)}, u32[]{:S(2)}, u32[]{:S(2)}) async-start(bf16[16,8,8,7168]{3,2,1,0:T(8,128)(2,1)} %stack.2), calls=%async_computation | async-start | bytes 29360128 | tf_op jit(solution)/shard_map/all_to_all | solution.py:83
  26.8 0.0 reduce-scatter.2.cloned.1.call-start
  26.9 0.2 multiply_cosine_fusion
  27.1 0.1 copy.43
  27.2 0.1 copy.42
  27.4 0.1 copy.59
  27.5 0.8 pad_maximum_fusion
  28.3 3.9 collective-permute-start.1
  32.3 4.0 collective-permute-start
  36.9 4.7 convolution_convert_fusion
  41.6 1.4 copy.45
  43.1 0.7 subtract_convert_fusion
  43.8 0.3 fusion.15
  44.1 1.1 constant_dynamic-slice_fusion.1
  45.2 0.2 copy.58
  45.4 0.2 copy.60
  45.6 329.3 %collective-permute-done = bf16[256,576]{1,0:T(8,128)(2,1)} collective-permute-done((bf16[256,576]{1,0:T(8,128)(2,1)}, bf16[256,576]{1,0:T(8,128)(2,1)}, u32[]{:S(2)}, u32[]{:S(2)}) %collective-permute-start) | collective-permute-done | bytes 294944 | tf_op jit(solution)/shard_map/ppermute | solution.py:10
  374.9 0.1 broadcast_select_fusion
  375.0 1.1 maximum_maximum_fusion
  376.1 6.1 %fusion.2 = f32[768,256,8]{1,0,2:T(8,128)} fusion(bf16[8,128,512]{2,1,0:T(8,128)(2,1)S(1)} %copy-done, bf16[768,576]{1,0:T(8,128)(2,1)} %maximum_maximum_fusion, bf16[256,8,192]{0,2,1:T(8,128)(2,1)S(1)} %bitcast.32), kind=kOutput, calls=%fused_computation.6 | convolution fusion | flops 1880096768 | bytes 8650752 | tf_op jit(solution)/shard_map/thl,kl->htk/dot_general | solution.py:62
  382.2 4.0 bitcast_select_fusion
  386.3 2.6 copy-done.2
  388.9 1.1 fusion.32
  390.0 0.0 copy-done.4
  390.1 0.3 copy-done.6
  390.4 7.3 %fusion.9 = bf16[8,256,128]{1,2,0:T(8,128)(2,1)S(1)} fusion(bf16[8,512,128]{2,1,0:T(8,128)(2,1)S(1)} %copy-done.6, f32[8,256]{1,0:T(8,128)S(1)} %fusion.32, bf16[768,576]{1,0:T(8,128)(2,1)S(1)} %copy-done.4, f32[8,256,768]{1,2,0:T(8,128)} %copy-done.2), kind=kOutput, calls=%fused_computation.12 | convolution fusion | flops 1885080320 | bytes 14950400 | tf_op jit(solution)/shard_map/thl,hlv->thv/dot_general | solution.py:79
  397.7 7.6 %copy.51 = bf16[16,8,8,7168]{3,2,0,1:T(8,128)(2,1)S(1)} copy(bf16[16,8,8,7168]{3,2,1,0:T(8,128)(2,1)} %all-to-all-done) | data formatting | bytes 29360128 | tf_op jit(solution)/shard_map/all_to_all | solution.py:83
  405.3 6.3 %fusion.33 = f32[256,7168]{1,0:T(8,128)} fusion(bf16[256,1024]{0,1:T(8,128)(2,1)S(1)} %bitcast.33, bf16[1024,7168]{1,0:T(8,128)(2,1)S(1)} %bitcast.30), kind=kOutput, calls=%fused_computation.53 | convolution fusion | flops 3758096384 | bytes 22544384 | tf_op jit(solution)/shard_map/dot_general | solution.py:87
  411.7 0.0 reduce-scatter.2.cloned.1.call-update
  411.7 66.1 %reduce-scatter.2.cloned.1.call-done = f32[256,896]{1,0:T(8,128)} async-done(((f32[256,7168]{1,0:T(8,128)}), f32[256,896]{1,0:T(8,128)}) %reduce-scatter.2.cloned.1.call-update) | async-done | bytes 917520 | tf_op jit(solution)/shard_map/reduce_scatter | solution.py:88
  477.8 2.0 convert_element_type.54
  (24 shorter events, 0.2 us)
Async XLA Ops:
  6.5 369.6 %copy-start = (bf16[8,128,512]{2,1,0:T(8,128)(2,1)S(1)}, bf16[8,128,512]{2,1,0:T(8,128)(2,1)}, u32[]{:S(2)}) copy-start(bf16[8,128,512]{2,1,0:T(8,128)(2,1)} %param.13) | copy-start | bytes 3145732
  14.9 12.0 %copy-start.3 = (bf16[256,576]{0,1:T(8,128)(2,1)S(1)}, bf16[256,576]{0,1:T(8,128)(2,1)}, u32[]{:S(2)}) copy-start(bf16[256,576]{0,1:T(8,128)(2,1)} %param.9) | copy-start | bytes 884740
  14.9 12.5 %slice-start = ((bf16[256,576]{0,1:T(8,128)(2,1)}), bf16[256,512]{0,1:T(8,128)(2,1)S(1)}, s32[]{:S(2)}) async-start(bf16[256,576]{0,1:T(8,128)(2,1)} %param.9), calls=%async_computation.3 | async-start | bytes 524288 | tf_op jit(solution)/shard_map/slice | solution.py:46
  14.9 22.1 %copy-start.7 = (bf16[256,1536]{1,0:T(8,128)(2,1)S(1)}, bf16[256,1536]{1,0:T(8,128)(2,1)}, u32[]{:S(2)}) copy-start(bf16[256,1536]{1,0:T(8,128)(2,1)} %param.8) | copy-start | bytes 2359300
  14.9 382.9 %all-to-all-start = ((bf16[16,8,8,7168]{3,2,1,0:T(8,128)(2,1)}), bf16[16,8,8,7168]{3,2,1,0:T(8,128)(2,1)}, u32[]{:S(2)}, u32[]{:S(2)}) async-start(bf16[16,8,8,7168]{3,2,1,0:T(8,128)(2,1)} %stack.2), calls=%async_computation | async-start | bytes 29360128 | tf_op jit(solution)/shard_map/all_to_all | solution.py:83
  26.8 451.0 %reduce-scatter.2.cloned.1.call-start = ((), (), s32[]{:S(2)}) async-start(), calls=%async_computation.2 | async-start | bytes 8257536 | tf_op jit(solution)/shard_map/reduce_scatter | solution.py:88
  28.3 346.6 %collective-permute-start.1 = (bf16[256,576]{1,0:T(8,128)(2,1)}, bf16[256,576]{1,0:T(8,128)(2,1)}, u32[]{:S(2)}, u32[]{:S(2)}) collective-permute-start(bf16[256,576]{1,0:T(8,128)(2,1)} %pad_maximum_fusion), channel_id=1, source_target_pairs={{0,16},{16,32},{32,48},{48,64},{64,80},{80,96},{96,112},{112,128},... | collective-permute-start | bytes 884744 | tf_op jit(solution)/shard_map/ppermute | solution.py:10
  32.3 342.6 %collective-permute-start = (bf16[256,576]{1,0:T(8,128)(2,1)}, bf16[256,576]{1,0:T(8,128)(2,1)}, u32[]{:S(2)}, u32[]{:S(2)}) collective-permute-start(bf16[256,576]{1,0:T(8,128)(2,1)} %pad_maximum_fusion), channel_id=1, source_target_pairs={{0,32},{16,48},{32,64},{48,80},{64,96},{80,112},{96,128},{112,144}... | collective-permute-start | bytes 884744 | tf_op jit(solution)/shard_map/ppermute | solution.py:10
  375.0 7.2 %copy-start.5 = (bf16[256,8,32]{0,2,1:T(8,128)(2,1)S(1)}, bf16[256,8,32]{0,2,1:T(8,128)(2,1)}, u32[]{:S(2)}) copy-start(bf16[256,8,32]{0,2,1:T(8,128)(2,1)} %get-tuple-element.6) | copy-start | bytes 393220
  386.2 2.6 copy-start.2
  388.9 1.2 copy-start.4
  388.9 1.5 copy-start.6
  405.3 74.4 %copy-start.1 = (bf16[8,128,512]{2,1,0:T(8,128)(2,1)S(1)}, bf16[8,128,512]{2,1,0:T(8,128)(2,1)}, u32[]{:S(2)}) copy-start(bf16[8,128,512]{2,1,0:T(8,128)(2,1)} %param.13) | copy-start | bytes 3145732
Sparse Core Ops, SparseCore 0:
  411.8 65.8 reduce-scatter.1
